TPU v7x, 256 devices: a whole 4x4x8 slice. The times are simulated.
256 devices in a mesh: section: 4 (over x), expert: 32 (over z, y), mp: 2 (over core).
Axes of the slice: x: 4, y: 4, z: 8, core: 2. Of those that a mesh axis runs over, the one named last changes fastest.
Arguments:
- out_grad: bfloat16 [4, 4096, 4096], P('section', 'expert', 'mp'), may hold values from -6 to 6
- expert_ids: int32 [4, 4096, 2], P('section', 'expert'), may hold values from 0 to 31, all different within a row; in each aligned block of 128 rows (0 to 127, 128 to 255, ..., all dimensions but the last counted through in order) at most 16 rows name the same one
- gate_codes: int32 [4, 4096, 2], P('section', 'expert'), may hold values from 1 to 255
- up_weight: bfloat16 [4, 32, 4096, 1024], P('section', 'expert', None, 'mp'), may hold values from -0.09375 to 0.09375
- down_weight: bfloat16 [4, 32, 1024, 4096], P('section', 'expert', 'mp'), may hold values from -0.1875 to 0.1875
- pre_act: bfloat16 [4, 32, 512, 1024], P('section', 'expert', None, 'mp'), may hold values from -6 to 6
- conv_grad: bfloat16 [4, 4096, 4096], P('section', 'expert', 'mp'), may hold values from -6 to 6
- conv_input: bfloat16 [4, 4096, 4096], P('section', 'expert', 'mp'), may hold values from -0.09375 to 0.09375
- conv_weight: float32 [4, 4, 4096], P('section', None, 'mp'), may hold values from -3 to 3
- in_proj: bfloat16 [4, 4096, 4096], P('section', 'expert', 'mp'), may hold values from -0.09375 to 0.09375
Outputs:
- residual_to_previous: bfloat16 [4, 4096, 4096], P('section', 'expert', 'mp')
- kernel_grad: float32 [4, 4, 4096], P('section', None, 'mp')
Inputs may be any that keep to these rules, and one draw needn't show every extreme that they name: `expert_ids`: each token names two different experts; in every section, the tokens of one block of 128 name no expert more than 16 times, a bound that some block reaches.
All inputs are finite; a program needn't handle non-finite values.
Results may differ from a plain program's by a relative error of at most 0.0044.
Values may be sent and summed in bfloat16 or wider, within the bound.
A program may use at most 128 MiB of HBM per device.

v0:
```python
import jax
import jax.numpy as jnp
from jax import lax
from jax.sharding import PartitionSpec as P


def shifted(array, axis, by):
    size = lax.axis_size(axis)
    pairs = [(i, i + by) for i in range(size) if 0 <= i + by < size]
    return lax.ppermute(array, axis, pairs)


def silu_slope(pre_value):
    sig = jax.nn.sigmoid(pre_value)
    return sig * (1.0 + pre_value * (1.0 - sig))


def gated_rows(gates, rows, tok_rows):
    scaled = (gates[:, :, None] * rows.astype(jnp.float32)[:, None, :]).astype(jnp.bfloat16)
    return scaled.reshape(tok_rows * 2, rows.shape[1])


def fill_buffer(scaled, target, experts, capacity):
    width = scaled.shape[1]
    buffer = jnp.zeros((experts * capacity, width), jnp.bfloat16).at[target].set(scaled)
    return buffer.reshape(experts, capacity, width)


def shards(
    out_grad,
    expert_ids,
    gate_codes,
    up_weight,
    down_weight,
    pre_act,
    conv_grad,
    conv_input,
    conv_weight,
    in_proj,
):
    grad_rows = out_grad[0]
    route_ids = expert_ids[0]
    tok_rows = grad_rows.shape[0]
    experts = lax.axis_size("expert")
    capacity = pre_act.shape[2] // experts
    gates = gate_codes[0].astype(jnp.float32) / 256.0
    flat_ids = route_ids.reshape(tok_rows * 2)
    onehot = (flat_ids[:, None] == jnp.arange(experts, dtype=jnp.int32)[None, :]).astype(jnp.int32)
    before = jnp.cumsum(onehot, axis=0) - onehot
    position = jnp.sum(before * onehot, axis=1)
    target = flat_ids * capacity + position
    whole_rows = lax.all_gather(grad_rows, "mp", axis=1, tiled=True)
    buffer = fill_buffer(gated_rows(gates, whole_rows, tok_rows), target, experts, capacity)
    arrived = lax.all_to_all(buffer, "expert", split_axis=0, concat_axis=0, tiled=True)
    slot_rows = arrived.reshape(experts * capacity, whole_rows.shape[1])
    w_down = down_weight[0, 0]
    w_up = up_weight[0, 0]
    pre_slots = pre_act[0, 0].astype(jnp.float32)
    hidden = lax.dot_general(
        slot_rows, w_down, (((1,), (1,)), ((), ())), preferred_element_type=jnp.float32
    )
    pre_grad = (hidden * silu_slope(pre_slots)).astype(jnp.bfloat16)
    partial_value = lax.dot_general(
        pre_grad, w_up, (((1,), (1,)), ((), ())), preferred_element_type=jnp.float32
    )
    share = lax.psum_scatter(partial_value, "mp", scatter_dimension=1, tiled=True).astype(
        jnp.bfloat16
    )
    returned = lax.all_to_all(
        share.reshape(experts, capacity, share.shape[1]),
        "expert",
        split_axis=0,
        concat_axis=0,
        tiled=True,
    )
    picked = returned.reshape(experts * capacity, grad_rows.shape[1])[target]
    picked = picked.astype(jnp.float32).reshape(tok_rows, 2, grad_rows.shape[1])
    moe_total = grad_rows.astype(jnp.float32) + picked[:, 0, :] + picked[:, 1, :]
    grads_here = conv_grad[0]
    inputs_here = conv_input[0]
    taps = conv_weight[0]
    kernel_size = taps.shape[0]
    next_rows = shifted(grads_here[: kernel_size - 1], "expert", -1)
    prev_rows = shifted(inputs_here[tok_rows - kernel_size + 1 :], "expert", 1)
    grad_ext = jnp.concatenate([grads_here, next_rows], axis=0).astype(jnp.float32)
    input_ext = jnp.concatenate([prev_rows, inputs_here], axis=0).astype(jnp.float32)
    grad_local = grads_here.astype(jnp.float32)
    conv_result = jnp.zeros(grads_here.shape, jnp.float32)
    tap_terms = []
    for tap in range(kernel_size):
        start = kernel_size - 1 - tap
        conv_result = conv_result + taps[tap][None, :] * grad_ext[start : start + tok_rows]
        tap_terms.append(jnp.sum(grad_local * input_ext[tap : tap + tok_rows], axis=0))
    input_grad = conv_result.astype(jnp.bfloat16)
    tap_grads = lax.psum(jnp.stack(tap_terms), "expert")
    w_proj = in_proj[0]
    proj_partial = lax.dot_general(
        input_grad,
        lax.all_gather(w_proj, "expert", axis=0, tiled=True),
        (((1,), (1,)), ((), ())),
        preferred_element_type=jnp.float32,
    )
    proj_share = lax.psum_scatter(proj_partial, "mp", scatter_dimension=1, tiled=True)
    residual = (moe_total + proj_share).astype(jnp.bfloat16)
    sent_residual = shifted(residual, "section", -1)
    return (sent_residual[None], tap_grads[None])


def solution(mesh):
    in_specs = (
        P("section", "expert", "mp"),
        P("section", "expert", None),
        P("section", "expert", None),
        P("section", "expert", None, "mp"),
        P("section", "expert", "mp", None),
        P("section", "expert", None, "mp"),
        P("section", "expert", "mp"),
        P("section", "expert", "mp"),
        P("section", None, "mp"),
        P("section", "expert", "mp"),
    )
    out_specs = (P("section", "expert", "mp"), P("section", None, "mp"))
    return jax.shard_map(shards, mesh=mesh, in_specs=in_specs, out_specs=out_specs, check_vma=False)
```

profile of v0, /device:TPU:6, one launch (start us, length us, event | category | flops | bytes accessed | tf_op | source)
XLA Modules:
  0.0 510.5 jit_solution(10965666901345054638)
XLA Ops:
  8.0 0.0 all-gather.5.cloned.1.call-start
  8.0 0.7 all-gather.5.cloned.1.call-update
  8.7 0.0 reduce-scatter.3.cloned.1.call-start
  8.8 0.8 copy.13
  9.6 0.1 eq.25
  9.7 0.1 eq.29
  9.8 0.7 broadcast_multiply_fusion
  10.5 0.1 copy.12
  10.6 0.1 mul.98
  10.8 0.6 reduce-window.6
  11.4 0.2 slice_reduce_fusion
  11.6 0.7 convert_multiply_fusion.5
  12.3 0.1 copy.16
  12.4 0.1 div.13
  12.6 0.1 fusion.39
  12.7 15.3 %all-gather.5.cloned.1.call-done = bf16[1,128,4096]{2,1,0:T(8,128)(2,1)} async-done(((bf16[1,128,2048]{2,1,0:T(8,128)(2,1)}), bf16[1,128,4096]{2,1,0:T(8,128)(2,1)}) %all-gather.5.cloned.1.call-update) | async-done | bytes 1048592 | tf_op jit(solution)/shard_map/all_gather | solution.py:52
  27.9 1.4 bitcast_convert_fusion
  29.4 4.4 mul.101
  33.7 6.1 %mul.102 = f32[256,4096]{1,0:T(8,128)} reshape(f32[128,2,4096]{2,1,0:T(2,128)} %mul.101) | data formatting | bytes 8388608 | tf_op jit(solution)/shard_map/mul | solution.py:19
  39.8 7.7 %scatter_custom_fusion = bf16[512,4096]{1,0:T(8,128)(2,1)} fusion(s32[256]{0:T(256)S(1)} %bitcast.99, f32[256,4096]{1,0:T(8,128)} %mul.102, f32[256]{0:T(256)S(1)} %div.13, bf16[]{:T(256)} %constant.7.clone.1), kind=kCustom, calls=%fused_computation.9 | custom fusion | flops 2097152 | bytes 8389634 | tf_op jit(solution)/shard_map/scatter | solution.py:25
  47.5 0.0 copy-start.5
  47.5 0.0 copy-start.6
  47.5 106.0 %all_to_all.10 = bf16[32,16,4096]{2,1,0:T(8,128)(2,1)S(1)} all-to-all(bf16[32,16,4096]{2,1,0:T(8,128)(2,1)} %bitcast.85), channel_id=1, replica_groups=mesh['section'=4,'expert'=32,'mp'=2] {'expert'}, dimensions={0} | all-to-all | bytes 8388608 | tf_op jit(solution)/shard_map/all_to_all | solution.py:54
  153.6 0.0 copy-done.5
  153.6 0.0 copy-done.6
  153.6 0.0 copy-start
  153.6 2.5 fusion.12
  156.1 0.0 copy-done
  156.1 5.6 %fusion.2 = f32[512,4096]{1,0:T(8,128)} fusion(bf16[512,512]{1,0:T(8,128)(2,1)S(1)} %fusion.12, bf16[1,1,4096,512]{3,2,1,0:T(8,128)(2,1)S(1)} %copy-done), kind=kOutput, calls=%fused_computation.4 | convolution fusion | flops 2147483648 | bytes 13107200 | tf_op jit(solution)/shard_map/dot_general | solution.py:63
  161.7 0.0 copy-start.1
  161.7 0.0 copy-start.4
  161.7 0.0 reduce-scatter.3.cloned.1.call-update
  161.8 0.0 all-gather.7.cloned.1.call-start
  161.8 0.5 all-gather.7.cloned.1.call-update
  162.3 0.4 copy-done.1
  162.8 1.3 collective-permute-start
  164.1 0.0 copy-done.4
  164.1 4.3 collective-permute-done
  168.4 0.1 maximum_convert_fusion
  168.5 12.6 %reduce-scatter.3.cloned.1.call-done = f32[512,2048]{1,0:T(8,128)} async-done(((f32[512,4096]{1,0:T(8,128)}), f32[512,2048]{1,0:T(8,128)}) %reduce-scatter.3.cloned.1.call-update) | async-done | bytes 4194320 | tf_op jit(solution)/shard_map/reduce_scatter | solution.py:66
  181.2 3.9 convert_element_type.68
  185.0 9.8 %all-to-all-start.1 = ((bf16[32,16,2048]{2,1,0:T(8,128)(2,1)}), bf16[32,16,2048]{2,1,0:T(8,128)(2,1)S(1)}, u32[]{:S(2)}, u32[]{:S(2)}) async-start(bf16[32,16,2048]{2,1,0:T(8,128)(2,1)} %bitcast.86), calls=%async_computation.2 | async-start | bytes 4194304 | tf_op jit(solution)/shard_map/all_to_all | solution.py:69
  194.8 0.0 reduce-scatter.5.cloned.1.call-start
  194.9 133.4 %all-gather.7.cloned.1.call-done = bf16[1,4096,2048]{2,1,0:T(8,128)(2,1)} async-done(((bf16[1,128,2048]{2,1,0:T(8,128)(2,1)}), bf16[1,4096,2048]{2,1,0:T(8,128)(2,1)}) %all-gather.7.cloned.1.call-update) | async-done | bytes 16777232 | tf_op jit(solution)/shard_map/all_gather | solution.py:99
  328.3 12.8 %fusion = f32[128,4096]{1,0:T(8,128)} fusion(bf16[1,4096,2048]{2,1,0:T(8,128)(2,1)} %all-gather.7.cloned.1.call-done, f32[131,2048]{1,0:T(8,128)S(1)} %maximum_convert_fusion, f32[2048]{0:T(1024)S(1)} %bitcast.93, f32[2048]{0:T(1024)S(1)} %bitcast.94, f32[2048]{0:T(1024)S(1)} %bitcast.92, f32[2048]{0:T(1024)S(1)} %bitcast.91), kind=kOutput, calls=%fused_computation.2 | convolution fusion | flops 2149580800 | bytes 23101440 | tf_op jit(solution)/shard_map/dot_general | solution.py:97
  341.1 0.0 reduce-scatter.5.cloned.1.call-update
  341.1 0.8 slice_bitcast_fusion
  341.9 2.1 collective-permute-start.2
  344.0 0.0 all-to-all-done.1
  344.0 1.4 gather_fusion
  345.4 1.3 reshape.97
  346.7 2.7 fusion.41
  349.4 0.0 copy-start.3
  349.4 4.0 reduce-scatter.5.cloned.1.call-done
  353.4 2.4 fusion.30
  355.8 2.8 collective-permute-start.1
  358.6 0.0 collective-permute-done.2
  358.7 0.0 copy-done.3
  358.7 0.1 maximum_convert_fusion.1
  358.8 0.0 copy-done.2
  358.8 0.6 fusion.20
  359.4 143.1 %psum.7 = f32[1,4,2048]{2,1,0:T(4,128)} all-reduce(f32[1,4,2048]{2,1,0:T(4,128)S(1)} %maximum_bitcast_fusion), channel_id=1, replica_groups=mesh['section'=4,'expert'=32,'mp'=2] {'expert'}, use_global_device_ids=true, to_apply=%region_10.11 | all-reduce | flops 8192 | bytes 65536 | tf_op jit(solution)/shard_map/psum | solution.py:95
  502.6 0.0 collective-permute-done.1
  502.6 0.8 copy.36
  (9 shorter events, 0.1 us)
Async XLA Ops:
  8.0 19.9 %all-gather.5.cloned.1.call-start = ((), (), s32[]{:S(2)}) async-start(), calls=%async_computation.6 | async-start | bytes 1572864 | tf_op jit(solution)/shard_map/all_gather | solution.py:52
  8.7 172.4 %reduce-scatter.3.cloned.1.call-start = ((), (), s32[]{:S(2)}) async-start(), calls=%async_computation.4 | async-start | bytes 12582912 | tf_op jit(solution)/shard_map/reduce_scatter | solution.py:66
  47.5 106.0 %copy-start.5 = (bf16[1,1,512,4096]{3,2,1,0:T(8,128)(2,1)S(1)}, bf16[1,1,512,4096]{3,2,1,0:T(8,128)(2,1)}, u32[]{:S(2)}) copy-start(bf16[1,1,512,4096]{3,2,1,0:T(8,128)(2,1)} %param.14) | copy-start | bytes 12582916
  47.5 106.0 %copy-start.6 = (bf16[1,1,512,512]{3,2,1,0:T(8,128)(2,1)S(1)}, bf16[1,1,512,512]{3,2,1,0:T(8,128)(2,1)}, u32[]{:S(2)}) copy-start(bf16[1,1,512,512]{3,2,1,0:T(8,128)(2,1)} %param.15) | copy-start | bytes 1572868
  153.6 2.6 copy-start
  161.7 1.0 copy-start.1
  161.7 2.4 copy-start.4
  161.8 166.5 %all-gather.7.cloned.1.call-start = ((), (), s32[]{:S(2)}) async-start(), calls=%async_computation.7 | async-start | bytes 17301504 | tf_op jit(solution)/shard_map/all_gather | solution.py:99
  162.8 5.6 %collective-permute-start = (bf16[3,2048]{1,0:T(4,128)(2,1)S(1)}, bf16[3,2048]{1,0:T(4,128)(2,1)S(1)}, u32[]{:S(2)}, u32[]{:S(2)}) collective-permute-start(bf16[3,2048]{1,0:T(4,128)(2,1)S(1)} %slice_bitcast_fusion.1), channel_id=1, source_target_pairs={{2,0},{4,2},{6,4},{8,6},{10,8},{12,10},{14,12},{16,14},{18,16},{20... | collective-permute-start | bytes 36872 | tf_op jit(solution)/shard_map/ppermute | solution.py:10
  185.0 159.0 %all-to-all-start.1 = ((bf16[32,16,2048]{2,1,0:T(8,128)(2,1)}), bf16[32,16,2048]{2,1,0:T(8,128)(2,1)S(1)}, u32[]{:S(2)}, u32[]{:S(2)}) async-start(bf16[32,16,2048]{2,1,0:T(8,128)(2,1)} %bitcast.86), calls=%async_computation.2 | async-start | bytes 4194304 | tf_op jit(solution)/shard_map/all_to_all | solution.py:69
  194.8 158.6 %reduce-scatter.5.cloned.1.call-start = ((), (), s32[]{:S(2)}) async-start(), calls=%async_computation.5 | async-start | bytes 3145728 | tf_op jit(solution)/shard_map/reduce_scatter | solution.py:103
  341.9 16.7 %collective-permute-start.2 = (bf16[3,2048]{1,0:T(4,128)(2,1)S(1)}, bf16[3,2048]{1,0:T(4,128)(2,1)S(1)}, u32[]{:S(2)}, u32[]{:S(2)}) collective-permute-start(bf16[3,2048]{1,0:T(4,128)(2,1)S(1)} %slice_bitcast_fusion), channel_id=1, source_target_pairs={{0,2},{2,4},{4,6},{6,8},{8,10},{10,12},{12,14},{14,16},{16,18},{18... | collective-permute-start | bytes 36872 | tf_op jit(solution)/shard_map/ppermute | solution.py:10
  349.4 9.3 %copy-start.3 = (bf16[1,128,2048]{2,1,0:T(8,128)(2,1)S(1)}, bf16[1,128,2048]{2,1,0:T(8,128)(2,1)}, u32[]{:S(2)}) copy-start(bf16[1,128,2048]{2,1,0:T(8,128)(2,1)} %param.17) | copy-start | bytes 1572868
  349.4 9.4 %copy-start.2 = (bf16[1,128,2048]{2,1,0:T(8,128)(2,1)S(1)}, bf16[1,128,2048]{2,1,0:T(8,128)(2,1)}, u32[]{:S(2)}) copy-start(bf16[1,128,2048]{2,1,0:T(8,128)(2,1)} %param.16) | copy-start | bytes 1572868
  355.8 146.7 %collective-permute-start.1 = (bf16[128,2048]{1,0:T(8,128)(2,1)S(1)}, bf16[128,2048]{1,0:T(8,128)(2,1)S(1)}, u32[]{:S(2)}, u32[]{:S(2)}) collective-permute-start(bf16[128,2048]{1,0:T(8,128)(2,1)S(1)} %fusion.30), channel_id=1, source_target_pairs={{64,0},{128,64},{192,128},{65,1},{129,65},{193,129},{66,2},{130,66... | collective-permute-start | bytes 1572872 | tf_op jit(solution)/shard_map/ppermute | solution.py:10
Sparse Core Ops, SparseCore 0:
  10.6 17.2 all-gather.4
  161.9 19.2 reduce-scatter.2
  341.3 12.0 reduce-scatter.4
Sparse Core Ops, SparseCore 1:
  165.1 163.1 all-gather.6
where the time goes:
time: 511 us; the launch traced here: 510 us
  blocking collectives  249 us (49%)
  waiting for transfers between devices  171 us (33%)
  matrix products  21 us (4%)
  local copies, waits for them, and re-layouts  19.6 us (4%)
  other arithmetic  18.5 us (4%)
  starting transfers between devices  16.1 us (3%)
  between operations  15.4 us (3%)
    psum x1, blocking collectives, shards(): tap_grads = lax.psum(jnp.stack(tap_terms), 'expert')  143 us
    all_gather x1, waiting for transfers between devices, shards(): lax.all_gather(w_proj, 'expert', axis=0, tiled=True)  133 us
    all_to_all x1, blocking collectives, shards(): lax.all_to_all(buffer, 'expert', split_axis=0, concat_axis=0, tiled=True)  106 us
    all_gather x1, waiting for transfers between devices, shards(): whole_rows = lax.all_gather(grad_rows, 'mp', axis=1, tiled=True)  15.3 us
    dot_general x1, matrix products, shards(): lax.dot_general(input_grad, lax.all_gather(w_proj, 'expert', axis=0, tile...  12.8 us
    reduce_scatter x1, waiting for transfers between devices, shards(): lax.psum_scatter(partial_value, 'mp', scatter_dimension=1, tiled=True)  12.6 us
    mul x2, local copies, waits for them, and re-layouts, gated_rows(): gates[:, :, None] * rows.astype(jnp.float32)[:, None, :]  10.4 us
  transfers between devices with their start and end apart: 8, of which 5 were waited for; matrix products, arithmetic and copies ran while one was open for 6% of the time, Pallas kernels for 0%

commit v1 on v0

--- a/solution.py
+++ b/solution.py
@@ -2,6 +2,11 @@
 import jax.numpy as jnp
 from jax import lax
 from jax.sharding import PartitionSpec as P
+
+
+def gather_and_add(x, axis):
+    parts = lax.all_gather(x, axis)
+    return jnp.sum(parts, axis=0)
 
 
 def shifted(array, axis, by):
@@ -92,7 +97,7 @@
         conv_result = conv_result + taps[tap][None, :] * grad_ext[start : start + tok_rows]
         tap_terms.append(jnp.sum(grad_local * input_ext[tap : tap + tok_rows], axis=0))
     input_grad = conv_result.astype(jnp.bfloat16)
-    tap_grads = lax.psum(jnp.stack(tap_terms), "expert")
+    tap_grads = gather_and_add(jnp.stack(tap_terms), "expert")
     w_proj = in_proj[0]
     proj_partial = lax.dot_general(
         input_grad,

time: 511 us -> 412 us (0.81)
  blocking collectives: 249 us -> 138 us
  waiting for transfers between devices: 171 us -> 180 us
    psum x1 -> x0, blocking collectives: 143 us -> none  [shards(): tap_grads = lax.psum(jnp.stack(tap_terms), 'expert')]
    all_gather x1, waiting for transfers between devices: 133 us -> 40 us  [shards(): lax.all_gather(w_proj, 'expert', axis=0, tiled=True)]
    all_gather x0 -> x1, waiting for transfers between devices: none -> 64.1 us  [gather_and_add(): parts = lax.all_gather(x, axis)]
    all_to_all x1, waiting for transfers between devices: 0.01 us -> 43.5 us  [shards(): lax.all_to_all(share.reshape(experts, capacity, share.shape[1]), 'expert'...]
    all_to_all x1, blocking collectives: 106 us -> 138 us  [shards(): lax.all_to_all(buffer, 'expert', split_axis=0, concat_axis=0, tiled=True)]
  transfers between devices with their start and end apart: 8 -> 9, of which waited for: 5 -> 7; matrix products, arithmetic and copies ran while one was open for 6% -> 14% of each run, Pallas kernels for 0% -> 0%
where the time goes in v1:
time: 412 us; the launch traced here: 411 us
  waiting for transfers between devices  180 us (44%)
  blocking collectives  138 us (33%)
  other arithmetic  21 us (5%)
  matrix products  20.9 us (5%)
  local copies, waits for them, and re-layouts  19.3 us (5%)
  starting transfers between devices  18 us (4%)
  between operations  14 us (3%)
    all_to_all x1, blocking collectives, shards(): lax.all_to_all(buffer, 'expert', split_axis=0, concat_axis=0, tiled=True)  138 us
    all_gather x1, waiting for transfers between devices, gather_and_add(): parts = lax.all_gather(x, axis)  64.1 us
    all_to_all x1, waiting for transfers between devices, shards(): lax.all_to_all(share.reshape(experts, capacity, share.shape[1]), 'expert'...  43.5 us
    all_gather x1, waiting for transfers between devices, shards(): lax.all_gather(w_proj, 'expert', axis=0, tiled=True)  40 us
    all_gather x1, waiting for transfers between devices, shards(): whole_rows = lax.all_gather(grad_rows, 'mp', axis=1, tiled=True)  14.5 us
    dot_general x1, matrix products, shards(): lax.dot_general(input_grad, lax.all_gather(w_proj, 'expert', axis=0, tile...  12.8 us
    mul x2, local copies, waits for them, and re-layouts, gated_rows(): gates[:, :, None] * rows.astype(jnp.float32)[:, None, :]  10.4 us
    reduce_scatter x1, waiting for transfers between devices, shards(): lax.psum_scatter(partial_value, 'mp', scatter_dimension=1, tiled=True)  10 us
  transfers between devices with their start and end apart: 9, of which 7 were waited for; matrix products, arithmetic and copies ran while one was open for 14% of the time, Pallas kernels for 0%

profile of v1, /device:TPU:6, one launch (start us, length us, event | category | flops | bytes accessed | tf_op | source)
XLA Modules:
  0.0 411.2 jit_solution(7926304286385347821)
XLA Ops:
  7.2 0.0 all-gather.8.cloned.1.call-start
  7.2 0.7 all-gather.8.cloned.1.call-update
  7.9 0.0 all-gather.10.cloned.1.call-start
  7.9 0.7 all-gather.10.cloned.1.call-update
  8.6 0.0 reduce-scatter.3.cloned.1.call-start
  8.7 0.8 copy.20
  9.5 0.1 eq.25
  9.6 0.1 eq.29
  9.8 0.7 broadcast_multiply_fusion
  10.4 0.1 copy.19
  10.6 0.1 mul.98
  10.7 0.6 reduce-window.6
  11.3 0.2 slice_reduce_fusion
  11.5 0.7 convert_multiply_fusion.5
  12.2 0.1 copy.23
  12.3 0.1 div.13
  12.5 0.1 fusion.39
  12.6 14.5 %all-gather.8.cloned.1.call-done = bf16[1,128,4096]{2,1,0:T(8,128)(2,1)} async-done(((bf16[1,128,2048]{2,1,0:T(8,128)(2,1)}), bf16[1,128,4096]{2,1,0:T(8,128)(2,1)}) %all-gather.8.cloned.1.call-update) | async-done | bytes 1048592 | tf_op jit(solution)/shard_map/all_gather | solution.py:57
  27.1 1.4 bitcast_convert_fusion
  28.6 4.3 %mul.101 = f32[128,2,4096]{2,1,0:T(2,128)} broadcast(f32[128,4096]{1,0:T(8,128)S(1)} %bitcast_convert_fusion), dimensions={0,2} | broadcast | bytes 6291456 | tf_op jit(solution)/shard_map/mul | solution.py:24
  32.9 6.1 %mul.102 = f32[256,4096]{1,0:T(8,128)} reshape(f32[128,2,4096]{2,1,0:T(2,128)} %mul.101) | data formatting | bytes 8388608 | tf_op jit(solution)/shard_map/mul | solution.py:24
  39.0 7.7 %scatter_custom_fusion = bf16[512,4096]{1,0:T(8,128)(2,1)} fusion(s32[256]{0:T(256)S(1)} %bitcast.101, f32[256,4096]{1,0:T(8,128)} %mul.102, f32[256]{0:T(256)S(1)} %div.13, bf16[]{:T(256)} %constant.7.clone.1), kind=kCustom, calls=%fused_computation.9 | custom fusion | flops 2097152 | bytes 8389634 | tf_op jit(solution)/shard_map/scatter | solution.py:30
  46.7 0.0 copy-start.4
  46.7 0.0 copy-start.5
  46.7 138.1 %all_to_all.10 = bf16[32,16,4096]{2,1,0:T(8,128)(2,1)S(1)} all-to-all(bf16[32,16,4096]{2,1,0:T(8,128)(2,1)} %bitcast.86), channel_id=1, replica_groups=mesh['section'=4,'expert'=32,'mp'=2] {'expert'}, dimensions={0} | all-to-all | bytes 8388608 | tf_op jit(solution)/shard_map/all_to_all | solution.py:59
  184.8 0.0 copy-done.4
  184.9 0.0 copy-done.5
  184.9 0.0 copy-start
  184.9 2.5 fusion.12
  187.4 0.0 copy-done
  187.4 5.6 %fusion.2 = f32[512,4096]{1,0:T(8,128)} fusion(bf16[512,512]{1,0:T(8,128)(2,1)S(1)} %fusion.12, bf16[1,1,4096,512]{3,2,1,0:T(8,128)(2,1)S(1)} %copy-done), kind=kOutput, calls=%fused_computation.4 | convolution fusion | flops 2147483648 | bytes 13107200 | tf_op jit(solution)/shard_map/dot_general | solution.py:68
  193.0 0.0 copy-start.1
  193.0 0.0 reduce-scatter.3.cloned.1.call-update
  193.0 0.0 reduce-scatter.5.cloned.1.call-start
  193.1 1.0 copy-done.1
  194.1 1.3 collective-permute-start
  195.4 0.0 copy-done.3
  195.4 4.6 %collective-permute-done = bf16[3,2048]{1,0:T(4,128)(2,1)S(1)} collective-permute-done((bf16[3,2048]{1,0:T(4,128)(2,1)S(1)}, bf16[3,2048]{1,0:T(4,128)(2,1)S(1)}, u32[]{:S(2)}, u32[]{:S(2)}) %collective-permute-start) | collective-permute-done | bytes 12320 | tf_op jit(solution)/shard_map/ppermute | solution.py:15
  200.0 0.1 maximum_convert_fusion
  200.2 40.0 %all-gather.10.cloned.1.call-done = bf16[1,4096,2048]{2,1,0:T(8,128)(2,1)} async-done(((bf16[1,128,2048]{2,1,0:T(8,128)(2,1)}), bf16[1,4096,2048]{2,1,0:T(8,128)(2,1)}) %all-gather.10.cloned.1.call-update) | async-done | bytes 16777232 | tf_op jit(solution)/shard_map/all_gather | solution.py:104
  240.2 12.8 %fusion = f32[128,4096]{1,0:T(8,128)} fusion(bf16[1,4096,2048]{2,1,0:T(8,128)(2,1)} %all-gather.10.cloned.1.call-done, f32[131,2048]{1,0:T(8,128)S(1)} %maximum_convert_fusion, f32[2048]{0:T(1024)S(1)} %bitcast.94, f32[2048]{0:T(1024)S(1)} %bitcast.95, f32[2048]{0:T(1024)S(1)} %bitcast.93, f32[2048]{0:T(1024)S(1)} %bitcast.92), kind=kOutput, calls=%fused_computation.2 | convolution fusion | flops 2149580800 | bytes 23101440 | tf_op jit(solution)/shard_map/dot_general | solution.py:102
  253.0 0.0 reduce-scatter.5.cloned.1.call-update
  253.0 0.0 copy-start.2
  253.0 10.0 %reduce-scatter.3.cloned.1.call-done = f32[512,2048]{1,0:T(8,128)} async-done(((f32[512,4096]{1,0:T(8,128)}), f32[512,2048]{1,0:T(8,128)}) %reduce-scatter.3.cloned.1.call-update) | async-done | bytes 4194320 | tf_op jit(solution)/shard_map/reduce_scatter | solution.py:71
  263.1 3.9 convert_element_type.68
  266.9 9.8 %all-to-all-start.1 = ((bf16[32,16,2048]{2,1,0:T(8,128)(2,1)}), bf16[32,16,2048]{2,1,0:T(8,128)(2,1)S(1)}, u32[]{:S(2)}, u32[]{:S(2)}) async-start(bf16[32,16,2048]{2,1,0:T(8,128)(2,1)} %bitcast.87), calls=%async_computation.2 | async-start | bytes 4194304 | tf_op jit(solution)/shard_map/all_to_all | solution.py:74
  276.8 0.0 all-gather.12.cloned.1.call-start
  276.8 0.0 copy-done.2
  276.8 3.9 collective-permute-start.2
  280.8 1.6 collective-permute-done.2
  282.4 0.1 maximum_convert_fusion.1
  282.6 0.6 fusion.20
  283.1 0.7 maximum_bitcast_fusion
  283.8 0.0 all-gather.12.cloned.1.call-update
  283.8 43.5 %all-to-all-done.1 = bf16[32,16,2048]{2,1,0:T(8,128)(2,1)S(1)} async-done(((bf16[32,16,2048]{2,1,0:T(8,128)(2,1)}), bf16[32,16,2048]{2,1,0:T(8,128)(2,1)S(1)}, u32[]{:S(2)}, u32[]{:S(2)}) %all-to-all-start.1) | async-done | bytes 2097184 | tf_op jit(solution)/shard_map/all_to_all | solution.py:74
  327.3 1.4 gather_fusion
  328.7 1.3 reshape.97
  330.0 2.6 fusion.41
  332.6 2.4 fusion.30
  335.1 2.8 collective-permute-start.1
  337.9 64.1 %all-gather.12.cloned.1.call-done = f32[32,4,2048]{2,1,0:T(4,128)} async-done(((f32[1,4,2048]{2,1,0:T(4,128)}), f32[32,4,2048]{2,1,0:T(4,128)}) %all-gather.12.cloned.1.call-update) | async-done | bytes 1048592 | tf_op jit(solution)/shard_map/all_gather | solution.py:8
  401.9 2.0 reduce_sum.62
  403.9 0.0 collective-permute-done.1
  403.9 0.8 copy.43
  (10 shorter events, 0.1 us)
Async XLA Ops:
  7.2 20.0 %all-gather.8.cloned.1.call-start = ((), (), s32[]{:S(2)}) async-start(), calls=%async_computation.6 | async-start | bytes 1572864 | tf_op jit(solution)/shard_map/all_gather | solution.py:57
  7.9 232.3 %all-gather.10.cloned.1.call-start = ((), (), s32[]{:S(2)}) async-start(), calls=%async_computation.7 | async-start | bytes 17301504 | tf_op jit(solution)/shard_map/all_gather | solution.py:104
  8.6 254.4 %reduce-scatter.3.cloned.1.call-start = ((), (), s32[]{:S(2)}) async-start(), calls=%async_computation.4 | async-start | bytes 12582912 | tf_op jit(solution)/shard_map/reduce_scatter | solution.py:71
  46.7 138.2 %copy-start.4 = (bf16[1,1,512,4096]{3,2,1,0:T(8,128)(2,1)S(1)}, bf16[1,1,512,4096]{3,2,1,0:T(8,128)(2,1)}, u32[]{:S(2)}) copy-start(bf16[1,1,512,4096]{3,2,1,0:T(8,128)(2,1)} %param.14) | copy-start | bytes 12582916
  46.7 138.2 %copy-start.5 = (bf16[1,1,512,512]{3,2,1,0:T(8,128)(2,1)S(1)}, bf16[1,1,512,512]{3,2,1,0:T(8,128)(2,1)}, u32[]{:S(2)}) copy-start(bf16[1,1,512,512]{3,2,1,0:T(8,128)(2,1)} %param.15) | copy-start | bytes 1572868
  184.9 2.6 copy-start
  193.0 1.1 copy-start.1
  193.0 2.4 copy-start.3
  193.0 139.6 %reduce-scatter.5.cloned.1.call-start = ((), (), s32[]{:S(2)}) async-start(), calls=%async_computation.5 | async-start | bytes 3145728 | tf_op jit(solution)/shard_map/reduce_scatter | solution.py:108
  194.1 6.0 %collective-permute-start = (bf16[3,2048]{1,0:T(4,128)(2,1)S(1)}, bf16[3,2048]{1,0:T(4,128)(2,1)S(1)}, u32[]{:S(2)}, u32[]{:S(2)}) collective-permute-start(bf16[3,2048]{1,0:T(4,128)(2,1)S(1)} %slice_bitcast_fusion.1), channel_id=1, source_target_pairs={{2,0},{4,2},{6,4},{8,6},{10,8},{12,10},{14,12},{16,14},{18,16},{20... | collective-permute-start | bytes 36872 | tf_op jit(solution)/shard_map/ppermute | solution.py:15
  253.0 23.8 %copy-start.2 = (bf16[1,128,2048]{2,1,0:T(8,128)(2,1)S(1)}, bf16[1,128,2048]{2,1,0:T(8,128)(2,1)}, u32[]{:S(2)}) copy-start(bf16[1,128,2048]{2,1,0:T(8,128)(2,1)} %param.17) | copy-start | bytes 1572868
  266.9 60.4 %all-to-all-start.1 = ((bf16[32,16,2048]{2,1,0:T(8,128)(2,1)}), bf16[32,16,2048]{2,1,0:T(8,128)(2,1)S(1)}, u32[]{:S(2)}, u32[]{:S(2)}) async-start(bf16[32,16,2048]{2,1,0:T(8,128)(2,1)} %bitcast.87), calls=%async_computation.2 | async-start | bytes 4194304 | tf_op jit(solution)/shard_map/all_to_all | solution.py:74
  276.8 125.2 %all-gather.12.cloned.1.call-start = ((), (), s32[]{:S(2)}) async-start(), calls=%async_computation.8 | async-start | bytes 1081344 | tf_op jit(solution)/shard_map/all_gather | solution.py:8
  276.8 5.6 %collective-permute-start.2 = (bf16[3,2048]{1,0:T(4,128)(2,1)S(1)}, bf16[3,2048]{1,0:T(4,128)(2,1)S(1)}, u32[]{:S(2)}, u32[]{:S(2)}) collective-permute-start(bf16[3,2048]{1,0:T(4,128)(2,1)S(1)} %slice_bitcast_fusion), channel_id=1, source_target_pairs={{0,2},{2,4},{4,6},{6,8},{8,10},{10,12},{12,14},{14,16},{16,18},{18... | collective-permute-start | bytes 36872 | tf_op jit(solution)/shard_map/ppermute | solution.py:15
  335.1 68.9 %collective-permute-start.1 = (bf16[128,2048]{1,0:T(8,128)(2,1)S(1)}, bf16[128,2048]{1,0:T(8,128)(2,1)S(1)}, u32[]{:S(2)}, u32[]{:S(2)}) collective-permute-start(bf16[128,2048]{1,0:T(8,128)(2,1)S(1)} %fusion.30), channel_id=1, source_target_pairs={{64,0},{128,64},{192,128},{65,1},{129,65},{193,129},{66,2},{130,66... | collective-permute-start | bytes 1572872 | tf_op jit(solution)/shard_map/ppermute | solution.py:15
Sparse Core Ops, SparseCore 0:
  9.8 17.2 all-gather.7
  29.7 210.4 all-gather.9
  242.7 20.2 reduce-scatter.2
  265.6 16.2 reduce-scatter.4
  284.8 117.0 all-gather.11
